TPU v7x, 512 devices: a whole 4x8x8 slice. The times are simulated.
512 devices in a mesh: dp: 4 (over y_lo), seq: 32 (over z, y_hi, core), tensor: 4 (over x).
Axes of the slice: x: 4, y: 8 (y_hi: 2, y_lo: 4; y = y_hi * 4 + y_lo), z: 8, core: 2. Of those that a mesh axis runs over, the one named last changes fastest.
Arguments:
- queries: bfloat16 [4, 16384, 512], P('dp', 'seq', 'tensor'), may hold values from -6 to 6
- values: bfloat16 [4, 16384, 512], P('dp', 'seq', 'tensor'), may hold values from -6 to 6
- filt: float32 [16384, 512], P('seq', 'tensor'), may hold values from -4 to 4
- w_out: bfloat16 [512, 4096], P('tensor'), may hold values from -0.375 to 0.375
- cotangent: bfloat16 [4, 16384, 4096], P('dp', 'seq', 'tensor'), may hold values from -6 to 6
Outputs:
- mixed: bfloat16 [4, 16384, 4096], P('dp', 'seq', 'tensor')
- grad_query: bfloat16 [4, 16384, 512], P('dp', 'seq', 'tensor')
- grad_value: bfloat16 [4, 16384, 512], P('dp', 'seq', 'tensor')
- grad_filt: float32 [16384, 512], P('seq', 'tensor')
All inputs are finite; a program needn't handle non-finite values.
Results may differ from a plain program's by a relative error of at most 0.024.
Values may be sent and summed in bfloat16 or wider, within the bound.
No kernel may reach another device: no remote copies, remote signals or barrier semaphores. Data moves between devices by JAX's collectives and lax.ppermute only.
A program may use at most 64 MiB of HBM per device.

v0:
```python
import math
import jax
import jax.numpy as jnp
from jax import lax
from jax.sharding import PartitionSpec as P

HIGHEST = lax.Precision.HIGHEST


def for_sending(array):
    return jax.tree.map(lambda a: a.astype(jnp.bfloat16) if a.dtype == jnp.float32 else a, array)


def angle_table(first, second, period):
    index = first[:, None] * second[None, :] % period
    angle = -2.0 * math.pi / period * index.astype(jnp.float32)
    return (jnp.cos(angle), jnp.sin(angle))


def product(table_real, table_imag, data_real, data_imag, form):

    def apply(left, right):
        return jnp.einsum(form, left, right, precision=HIGHEST)

    return (
        apply(table_real, data_real) - apply(table_imag, data_imag),
        apply(table_real, data_imag) + apply(table_imag, data_real),
    )


def split_length(length):
    levels = length.bit_length() - 1
    inner = 1 << levels // 2
    return (inner, length // inner)


def local_forward(data_real, data_imag, freq_index, total):
    pair, length, width = data_real.shape
    inner, outer = split_length(length)
    cos_t, sin_t = angle_table(freq_index, jnp.arange(length, dtype=jnp.int32), total)
    cos_t = cos_t[:, :, None]
    sin_t = sin_t[:, :, None]
    data_real, data_imag = (
        data_real * cos_t - data_imag * sin_t,
        data_real * sin_t + data_imag * cos_t,
    )
    data_real = data_real.reshape(pair, outer, inner, width)
    data_imag = data_imag.reshape(pair, outer, inner, width)
    outer_c, outer_s = angle_table(
        jnp.arange(outer, dtype=jnp.int32), jnp.arange(outer, dtype=jnp.int32), outer
    )
    data_real, data_imag = product(outer_c, outer_s, data_real, data_imag, "ab,ebcd->eacd")
    mid_c, mid_s = angle_table(
        jnp.arange(outer, dtype=jnp.int32), jnp.arange(inner, dtype=jnp.int32), length
    )
    mid_c = mid_c[None, :, :, None]
    mid_s = mid_s[None, :, :, None]
    data_real, data_imag = (
        data_real * mid_c - data_imag * mid_s,
        data_real * mid_s + data_imag * mid_c,
    )
    inner_c, inner_s = angle_table(
        jnp.arange(inner, dtype=jnp.int32), jnp.arange(inner, dtype=jnp.int32), inner
    )
    return product(inner_c, inner_s, data_real, data_imag, "ab,ecbd->ecad")


def local_inverse(spec_real, spec_imag, freq_index, total):
    pair, outer, inner, width = spec_real.shape
    length = outer * inner
    inner_c, inner_s = angle_table(
        jnp.arange(inner, dtype=jnp.int32), jnp.arange(inner, dtype=jnp.int32), inner
    )
    data_real, data_imag = product(
        inner_c / inner, -inner_s / inner, spec_real, spec_imag, "ab,ecbd->ecad"
    )
    mid_c, mid_s = angle_table(
        jnp.arange(outer, dtype=jnp.int32), jnp.arange(inner, dtype=jnp.int32), length
    )
    mid_c = mid_c[None, :, :, None]
    mid_s = mid_s[None, :, :, None]
    data_real, data_imag = (
        data_real * mid_c + data_imag * mid_s,
        data_imag * mid_c - data_real * mid_s,
    )
    outer_c, outer_s = angle_table(
        jnp.arange(outer, dtype=jnp.int32), jnp.arange(outer, dtype=jnp.int32), outer
    )
    data_real, data_imag = product(
        outer_c / outer, -outer_s / outer, data_real, data_imag, "ab,ebcd->eacd"
    )
    data_real = data_real.reshape(pair, length, width)
    data_imag = data_imag.reshape(pair, length, width)
    cos_t, sin_t = angle_table(freq_index, jnp.arange(length, dtype=jnp.int32), total)
    cos_t = cos_t[:, :, None]
    sin_t = sin_t[:, :, None]
    return (data_real * cos_t + data_imag * sin_t, data_imag * cos_t - data_real * sin_t)


def forward_transform(signal):
    count = lax.axis_size("seq")
    place = lax.axis_index("seq")
    length, width = signal.shape
    total = 2 * count * length
    pieces = lax.all_to_all(
        signal.reshape(count, length // count, width).astype(jnp.bfloat16),
        "seq",
        split_axis=0,
        concat_axis=0,
        tiled=True,
    ).astype(jnp.float32)
    cos_t, sin_t = angle_table(
        jnp.arange(2 * count, dtype=jnp.int32), jnp.arange(count, dtype=jnp.int32), 2 * count
    )
    mixed_real = jnp.einsum("ka,arc->krc", cos_t, pieces, precision=HIGHEST)
    mixed_imag = jnp.einsum("ka,arc->krc", sin_t, pieces, precision=HIGHEST)
    mixed_real, mixed_imag = (
        lax.all_to_all(
            for_sending(mixed_real), "seq", split_axis=0, concat_axis=1, tiled=True
        ).astype(mixed_real.dtype),
        lax.all_to_all(
            for_sending(mixed_imag), "seq", split_axis=0, concat_axis=1, tiled=True
        ).astype(mixed_imag.dtype),
    )
    freq_index = 2 * place + jnp.arange(2, dtype=jnp.int32)
    return (local_forward(mixed_real, mixed_imag, freq_index, total), freq_index)


def inverse_transform(spectrum, freq_index):
    count = lax.axis_size("seq")
    pair, outer, inner, width = spectrum[0].shape
    length = outer * inner
    total = 2 * count * length
    data_real, data_imag = local_inverse(spectrum[0], spectrum[1], freq_index, total)
    part_real, part_imag = (
        lax.all_to_all(
            for_sending(data_real), "seq", split_axis=1, concat_axis=0, tiled=True
        ).astype(data_real.dtype),
        lax.all_to_all(
            for_sending(data_imag), "seq", split_axis=1, concat_axis=0, tiled=True
        ).astype(data_imag.dtype),
    )
    cos_t, sin_t = angle_table(
        jnp.arange(2 * count, dtype=jnp.int32), jnp.arange(count, dtype=jnp.int32), 2 * count
    )
    signal = (
        jnp.einsum("ka,krc->arc", cos_t, part_real, precision=HIGHEST)
        + jnp.einsum("ka,krc->arc", sin_t, part_imag, precision=HIGHEST)
    ) / (2 * count)
    signal = lax.all_to_all(
        for_sending(signal), "seq", split_axis=0, concat_axis=0, tiled=True
    ).astype(signal.dtype)
    return signal.reshape(length, width)


def split_spec(spectrum, width):
    first = (spectrum[0][..., :width], spectrum[1][..., :width])
    second = (spectrum[0][..., width:], spectrum[1][..., width:])
    return (first, second)


def times_spec(left, right):
    return (left[0] * right[0] - left[1] * right[1], left[0] * right[1] + left[1] * right[0])


def conj_times(left, right):
    return (left[0] * right[0] + left[1] * right[1], left[0] * right[1] - left[1] * right[0])


def per_device(queries, values, filt, w_out, cotangent):
    query = queries[0].astype(jnp.float32)
    value = values[0].astype(jnp.float32)
    width = filt.shape[1]
    joined = jnp.concatenate([value, filt], axis=1)
    spectrum, freq_index = forward_transform(joined)
    value_spec, filt_spec = split_spec(spectrum, width)
    conv = inverse_transform(times_spec(value_spec, filt_spec), freq_index)
    gated = (query * conv).astype(jnp.bfloat16)
    partial_sum = jnp.dot(gated, w_out, preferred_element_type=jnp.float32)
    mixed = lax.psum_scatter(
        partial_sum.astype(jnp.bfloat16), "tensor", scatter_dimension=1, tiled=True
    )
    grad_gated = lax.dot_general(
        lax.all_gather(cotangent[0], "tensor", axis=1, tiled=True),
        w_out,
        (((1,), (1,)), ((), ())),
        preferred_element_type=jnp.float32,
    )
    grad_query = (grad_gated * conv).astype(jnp.bfloat16)
    grad_conv = grad_gated * query
    grad_spec = forward_transform(grad_conv)[0]
    back_value = conj_times(filt_spec, grad_spec)
    back_filt = conj_times(value_spec, grad_spec)
    both_spec = (
        jnp.concatenate([back_value[0], back_filt[0]], axis=3),
        jnp.concatenate([back_value[1], back_filt[1]], axis=3),
    )
    result = inverse_transform(both_spec, freq_index)
    grad_value = result[:, :width].astype(jnp.bfloat16)
    grad_filt = lax.psum(result[:, width:].astype(jnp.bfloat16), "dp").astype(jnp.float32)
    return (mixed[None], grad_query[None], grad_value[None], grad_filt)


def solution(mesh):
    placed = (
        P("dp", "seq", "tensor"),
        P("dp", "seq", "tensor"),
        P("seq", "tensor"),
        P("tensor", None),
        P("dp", "seq", "tensor"),
    )
    return jax.shard_map(
        per_device,
        mesh=mesh,
        in_specs=placed,
        out_specs=(
            P("dp", "seq", "tensor"),
            P("dp", "seq", "tensor"),
            P("dp", "seq", "tensor"),
            P("seq", "tensor"),
        ),
        check_vma=False,
    )
```

profile of v0, /device:TPU:1, one launch (start us, length us, event | category | flops | bytes accessed | tf_op | source)
XLA Modules:
  0.0 429.1 jit_solution(16543263097162809174)
XLA Ops:
  7.9 1.0 convert.18
  8.9 0.9 pad_maximum_fusion.6
  9.8 30.7 %all_to_all.128 = bf16[32,16,256]{2,1,0:T(8,128)(2,1)S(1)} all-to-all(bf16[32,16,256]{2,1,0:T(8,128)(2,1)S(1)} %bitcast.303), channel_id=1, replica_groups=mesh['dp'=4,'seq'=32,'tensor'=4] {'seq'}, dimensions={0} | all-to-all | bytes 524288 | tf_op jit(solution)/shard_map/all_to_all | solution.py:105
  41.2 1.1 copy.71
  42.3 5.8 %all-to-all-start.1 = ((bf16[64,16,256]{2,1,0:T(8,128)(2,1)}), bf16[64,16,256]{2,1,0:T(8,128)(2,1)S(1)}, u32[]{:S(2)}, u32[]{:S(2)}) async-start(bf16[64,16,256]{2,1,0:T(8,128)(2,1)} %copy.71), calls=%async_computation.1 | async-start | bytes 1048576 | tf_op jit(solution)/shard_map/all_to_all | solution.py:118
  48.8 1.1 copy.74
  49.9 14.1 %all-to-all-done.1 = bf16[64,16,256]{2,1,0:T(8,128)(2,1)S(1)} async-done(((bf16[64,16,256]{2,1,0:T(8,128)(2,1)}), bf16[64,16,256]{2,1,0:T(8,128)(2,1)S(1)}, u32[]{:S(2)}, u32[]{:S(2)}) %all-to-all-start.1) | async-done | bytes 524320 | tf_op jit(solution)/shard_map/all_to_all | solution.py:118
  64.0 9.6 %all-to-all-start.2 = ((bf16[64,16,256]{2,1,0:T(8,128)(2,1)}), bf16[64,16,256]{2,1,0:T(8,128)(2,1)}, u32[]{:S(2)}, u32[]{:S(2)}) async-start(bf16[64,16,256]{2,1,0:T(8,128)(2,1)} %copy.74), calls=%async_computation.2 | async-start | bytes 1048576 | tf_op jit(solution)/shard_map/all_to_all | solution.py:121
  74.3 15.0 %all-to-all-done.2 = bf16[64,16,256]{2,1,0:T(8,128)(2,1)} async-done(((bf16[64,16,256]{2,1,0:T(8,128)(2,1)}), bf16[64,16,256]{2,1,0:T(8,128)(2,1)}, u32[]{:S(2)}, u32[]{:S(2)}) %all-to-all-start.2) | async-done | bytes 524320 | tf_op jit(solution)/shard_map/all_to_all | solution.py:121
  89.3 1.2 convert.22
  90.5 2.4 fusion.61
  92.9 2.4 fusion.65
  95.2 2.4 fusion.7
  97.7 3.8 multiply_subtract_fusion
  101.5 4.3 fusion.58
  105.8 9.8 %all-to-all-start.6 = ((bf16[32,16,128]{2,1,0:T(8,128)(2,1)}), bf16[32,16,128]{2,1,0:T(8,128)(2,1)S(1)}, u32[]{:S(2)}, u32[]{:S(2)}) async-start(bf16[32,16,128]{2,1,0:T(8,128)(2,1)} %bitcast.55), calls=%async_computation.7 | async-start | bytes 262144 | tf_op jit(solution)/shard_map/all_to_all | solution.py:105
  115.6 2.6 fusion.34
  118.2 9.6 %all-to-all-done.6 = bf16[32,16,128]{2,1,0:T(8,128)(2,1)S(1)} async-done(((bf16[32,16,128]{2,1,0:T(8,128)(2,1)}), bf16[32,16,128]{2,1,0:T(8,128)(2,1)S(1)}, u32[]{:S(2)}, u32[]{:S(2)}) %all-to-all-start.6) | async-done | bytes 131104 | tf_op jit(solution)/shard_map/all_to_all | solution.py:105
  129.2 4.6 %all-to-all-start.7 = ((bf16[64,16,128]{2,1,0:T(8,128)(2,1)}), bf16[64,16,128]{2,1,0:T(8,128)(2,1)}, u32[]{:S(2)}, u32[]{:S(2)}) async-start(bf16[64,16,128]{2,1,0:T(8,128)(2,1)} %copy.96), calls=%async_computation.8 | async-start | bytes 524288 | tf_op jit(solution)/shard_map/all_to_all | solution.py:118
  133.9 3.8 fusion.5
  139.1 8.6 %all-to-all-done.7 = bf16[64,16,128]{2,1,0:T(8,128)(2,1)} async-done(((bf16[64,16,128]{2,1,0:T(8,128)(2,1)}), bf16[64,16,128]{2,1,0:T(8,128)(2,1)}, u32[]{:S(2)}, u32[]{:S(2)}) %all-to-all-start.7) | async-done | bytes 262176 | tf_op jit(solution)/shard_map/all_to_all | solution.py:118
  147.7 5.8 %all-to-all-start.8 = ((bf16[64,16,128]{2,1,0:T(8,128)(2,1)}), bf16[64,16,128]{2,1,0:T(8,128)(2,1)S(1)}, u32[]{:S(2)}, u32[]{:S(2)}) async-start(bf16[64,16,128]{2,1,0:T(8,128)(2,1)} %copy.99), calls=%async_computation.9 | async-start | bytes 524288 | tf_op jit(solution)/shard_map/all_to_all | solution.py:121
  153.5 1.6 fusion.30
  155.1 1.6 fusion.4
  156.8 1.0 convert.23
  157.8 9.4 %all-to-all-done.8 = bf16[64,16,128]{2,1,0:T(8,128)(2,1)S(1)} async-done(((bf16[64,16,128]{2,1,0:T(8,128)(2,1)}), bf16[64,16,128]{2,1,0:T(8,128)(2,1)S(1)}, u32[]{:S(2)}, u32[]{:S(2)}) %all-to-all-start.8) | async-done | bytes 262176 | tf_op jit(solution)/shard_map/all_to_all | solution.py:121
  167.2 1.3 fusion.72
  168.5 1.3 fusion.76
  169.8 1.3 fusion.12
  171.1 1.4 multiply_subtract_fusion.3
  172.6 0.9 fusion.48
  173.5 0.9 fusion.44
  174.4 0.9 fusion.9
  175.3 1.4 multiply_subtract_fusion.2
  177.4 1.1 fusion.36
  178.4 1.1 fusion.37
  179.5 1.1 convolution_add_fusion.1
  180.6 1.4 add_bitcast_fusion
  182.0 1.7 fusion.28
  183.7 1.7 fusion.24
  185.4 1.7 fusion.3
  187.2 1.9 fusion.2
  190.4 1.1 fusion.21
  191.5 1.4 copy.116
  192.9 5.8 %all-to-all-start.10 = ((bf16[2,512,256]{2,0,1:T(2,128)(2,1)}), bf16[2,512,256]{2,0,1:T(2,128)(2,1)S(1)}, u32[]{:S(2)}, u32[]{:S(2)}) async-start(bf16[2,512,256]{2,0,1:T(2,128)(2,1)} %copy.116), calls=%async_computation.11 | async-start | bytes 1048576 | tf_op jit(solution)/shard_map/all_to_all | solution.py:139
  198.7 2.4 copy.113
  203.8 10.6 %all-to-all-done.10 = bf16[2,512,256]{2,0,1:T(2,128)(2,1)S(1)} async-done(((bf16[2,512,256]{2,0,1:T(2,128)(2,1)}), bf16[2,512,256]{2,0,1:T(2,128)(2,1)S(1)}, u32[]{:S(2)}, u32[]{:S(2)}) %all-to-all-start.10) | async-done | bytes 524320 | tf_op jit(solution)/shard_map/all_to_all | solution.py:139
  214.5 9.3 %all-to-all-start.9 = ((bf16[2,512,256]{2,0,1:T(2,128)(2,1)}), bf16[2,512,256]{2,0,1:T(2,128)(2,1)}, u32[]{:S(2)}, u32[]{:S(2)}) async-start(bf16[2,512,256]{2,0,1:T(2,128)(2,1)} %copy.113), calls=%async_computation.10 | async-start | bytes 1048576 | tf_op jit(solution)/shard_map/all_to_all | solution.py:136
  227.1 1.0 copy.91
  228.1 11.6 %all-to-all-done.9 = bf16[2,512,256]{2,0,1:T(2,128)(2,1)} async-done(((bf16[2,512,256]{2,0,1:T(2,128)(2,1)}), bf16[2,512,256]{2,0,1:T(2,128)(2,1)}, u32[]{:S(2)}, u32[]{:S(2)}) %all-to-all-start.9) | async-done | bytes 524320 | tf_op jit(solution)/shard_map/all_to_all | solution.py:136
  239.7 9.6 %all-to-all-start.4 = ((bf16[2,512,128]{2,0,1:T(2,128)(2,1)}), bf16[2,512,128]{2,0,1:T(2,128)(2,1)S(1)}, u32[]{:S(2)}, u32[]{:S(2)}) async-start(bf16[2,512,128]{2,0,1:T(2,128)(2,1)} %copy.91), calls=%async_computation.4 | async-start | bytes 524288 | tf_op jit(solution)/shard_map/all_to_all | solution.py:139
  249.3 1.0 copy.88
  251.1 1.1 copy.114
  253.0 9.8 %all-to-all-done.4 = bf16[2,512,128]{2,0,1:T(2,128)(2,1)S(1)} async-done(((bf16[2,512,128]{2,0,1:T(2,128)(2,1)}), bf16[2,512,128]{2,0,1:T(2,128)(2,1)S(1)}, u32[]{:S(2)}, u32[]{:S(2)}) %all-to-all-start.4) | async-done | bytes 262176 | tf_op jit(solution)/shard_map/all_to_all | solution.py:139
  262.8 5.8 %all-to-all-start.3 = ((bf16[2,512,128]{2,0,1:T(2,128)(2,1)}), bf16[2,512,128]{2,0,1:T(2,128)(2,1)S(1)}, u32[]{:S(2)}, u32[]{:S(2)}) async-start(bf16[2,512,128]{2,0,1:T(2,128)(2,1)} %copy.88), calls=%async_computation.3 | async-start | bytes 524288 | tf_op jit(solution)/shard_map/all_to_all | solution.py:136
  270.4 11.9 %all-to-all-done.3 = bf16[2,512,128]{2,0,1:T(2,128)(2,1)S(1)} async-done(((bf16[2,512,128]{2,0,1:T(2,128)(2,1)}), bf16[2,512,128]{2,0,1:T(2,128)(2,1)S(1)}, u32[]{:S(2)}, u32[]{:S(2)}) %all-to-all-start.3) | async-done | bytes 262176 | tf_op jit(solution)/shard_map/all_to_all | solution.py:136
  282.3 5.8 %all-to-all-start.11 = ((bf16[32,16,256]{2,1,0:T(8,128)(2,1)}), bf16[32,16,256]{2,1,0:T(8,128)(2,1)S(1)}, u32[]{:S(2)}, u32[]{:S(2)}) async-start(bf16[32,16,256]{2,1,0:T(8,128)(2,1)} %copy.119), calls=%async_computation.12 | async-start | bytes 524288 | tf_op jit(solution)/shard_map/all_to_all | solution.py:150
  290.2 11.6 %all-to-all-done.11 = bf16[32,16,256]{2,1,0:T(8,128)(2,1)S(1)} async-done(((bf16[32,16,256]{2,1,0:T(8,128)(2,1)}), bf16[32,16,256]{2,1,0:T(8,128)(2,1)S(1)}, u32[]{:S(2)}, u32[]{:S(2)}) %all-to-all-start.11) | async-done | bytes 262176 | tf_op jit(solution)/shard_map/all_to_all | solution.py:150
  301.8 5.8 %all-to-all-start.5 = ((bf16[32,16,128]{2,1,0:T(8,128)(2,1)}), bf16[32,16,128]{2,1,0:T(8,128)(2,1)S(1)}, u32[]{:S(2)}, u32[]{:S(2)}) async-start(bf16[32,16,128]{2,1,0:T(8,128)(2,1)} %copy.94), calls=%async_computation.5 | async-start | bytes 262144 | tf_op jit(solution)/shard_map/all_to_all | solution.py:150
  308.4 11.5 %all-to-all-done.5 = bf16[32,16,128]{2,1,0:T(8,128)(2,1)S(1)} async-done(((bf16[32,16,128]{2,1,0:T(8,128)(2,1)}), bf16[32,16,128]{2,1,0:T(8,128)(2,1)S(1)}, u32[]{:S(2)}, u32[]{:S(2)}) %all-to-all-start.5) | async-done | bytes 131104 | tf_op jit(solution)/shard_map/all_to_all | solution.py:150
  320.0 3.2 convolution_convert_fusion
  323.9 41.7 %all-reduce.2.cloned.1.call-done = bf16[512,128]{1,0:T(8,128)(2,1)} async-done(((bf16[512,128]{1,0:T(8,128)(2,1)}), bf16[512,128]{1,0:T(8,128)(2,1)}) %all-reduce.2.cloned.1.call-update) | async-done | bytes 131088 | tf_op jit(solution)/shard_map/psum | solution.py:200
  365.7 1.6 convert_element_type.305
  367.3 55.0 %reduce-scatter.2.cloned.1.call-done = bf16[512,1024]{1,0:T(8,128)(2,1)} async-done(((bf16[512,4096]{1,0:T(8,128)(2,1)}), bf16[512,1024]{1,0:T(8,128)(2,1)}) %reduce-scatter.2.cloned.1.call-update) | async-done | bytes 1048592 | tf_op jit(solution)/shard_map/reduce_scatter | solution.py:180
  (64 shorter events, 20.3 us)
Async XLA Ops:
  7.2 94.4 %copy-start = (bf16[128,4096]{1,0:T(8,128)(2,1)S(1)}, bf16[128,4096]{1,0:T(8,128)(2,1)}, u32[]{:S(2)}) copy-start(bf16[128,4096]{1,0:T(8,128)(2,1)} %param.8) | copy-start | bytes 3145732
  7.2 94.3 %all-gather.3.cloned.1.call-start = ((), (), s32[]{:S(2)}) async-start(), calls=%async_computation.15 | async-start | bytes 5242880 | tf_op jit(solution)/shard_map/all_gather | solution.py:184
  42.3 21.7 %all-to-all-start.1 = ((bf16[64,16,256]{2,1,0:T(8,128)(2,1)}), bf16[64,16,256]{2,1,0:T(8,128)(2,1)S(1)}, u32[]{:S(2)}, u32[]{:S(2)}) async-start(bf16[64,16,256]{2,1,0:T(8,128)(2,1)} %copy.71), calls=%async_computation.1 | async-start | bytes 1048576 | tf_op jit(solution)/shard_map/all_to_all | solution.py:118
  64.0 25.3 %all-to-all-start.2 = ((bf16[64,16,256]{2,1,0:T(8,128)(2,1)}), bf16[64,16,256]{2,1,0:T(8,128)(2,1)}, u32[]{:S(2)}, u32[]{:S(2)}) async-start(bf16[64,16,256]{2,1,0:T(8,128)(2,1)} %copy.74), calls=%async_computation.2 | async-start | bytes 1048576 | tf_op jit(solution)/shard_map/all_to_all | solution.py:121
  97.7 3.9 copy-start.4
  101.5 32.4 %copy-start.1 = (f32[2,32,16,256]{3,1,2,0:T(8,128)S(1)}, f32[2,32,16,256]{3,1,2,0:T(8,128)}, u32[]{:S(2)}) copy-start(f32[2,32,16,256]{3,1,2,0:T(8,128)} %get-tuple-element.11) | copy-start | bytes 3145732
  105.8 22.0 %all-to-all-start.6 = ((bf16[32,16,128]{2,1,0:T(8,128)(2,1)}), bf16[32,16,128]{2,1,0:T(8,128)(2,1)S(1)}, u32[]{:S(2)}, u32[]{:S(2)}) async-start(bf16[32,16,128]{2,1,0:T(8,128)(2,1)} %bitcast.55), calls=%async_computation.7 | async-start | bytes 262144 | tf_op jit(solution)/shard_map/all_to_all | solution.py:105
  129.2 18.4 %all-to-all-start.7 = ((bf16[64,16,128]{2,1,0:T(8,128)(2,1)}), bf16[64,16,128]{2,1,0:T(8,128)(2,1)}, u32[]{:S(2)}, u32[]{:S(2)}) async-start(bf16[64,16,128]{2,1,0:T(8,128)(2,1)} %copy.96), calls=%async_computation.8 | async-start | bytes 524288 | tf_op jit(solution)/shard_map/all_to_all | solution.py:118
  147.7 19.5 %all-to-all-start.8 = ((bf16[64,16,128]{2,1,0:T(8,128)(2,1)}), bf16[64,16,128]{2,1,0:T(8,128)(2,1)S(1)}, u32[]{:S(2)}, u32[]{:S(2)}) async-start(bf16[64,16,128]{2,1,0:T(8,128)(2,1)} %copy.99), calls=%async_computation.9 | async-start | bytes 524288 | tf_op jit(solution)/shard_map/all_to_all | solution.py:121
  169.8 5.5 %copy-start.2 = (f32[2,32,16,256]{3,2,1,0:T(8,128)S(1)}, f32[2,32,16,256]{3,2,1,0:T(8,128)}, u32[]{:S(2)}) copy-start(f32[2,32,16,256]{3,2,1,0:T(8,128)} %fusion.5) | copy-start | bytes 3145732
  192.9 21.6 %all-to-all-start.10 = ((bf16[2,512,256]{2,0,1:T(2,128)(2,1)}), bf16[2,512,256]{2,0,1:T(2,128)(2,1)S(1)}, u32[]{:S(2)}, u32[]{:S(2)}) async-start(bf16[2,512,256]{2,0,1:T(2,128)(2,1)} %copy.116), calls=%async_computation.11 | async-start | bytes 1048576 | tf_op jit(solution)/shard_map/all_to_all | solution.py:139
  214.5 25.2 %all-to-all-start.9 = ((bf16[2,512,256]{2,0,1:T(2,128)(2,1)}), bf16[2,512,256]{2,0,1:T(2,128)(2,1)}, u32[]{:S(2)}, u32[]{:S(2)}) async-start(bf16[2,512,256]{2,0,1:T(2,128)(2,1)} %copy.113), calls=%async_computation.10 | async-start | bytes 1048576 | tf_op jit(solution)/shard_map/all_to_all | solution.py:136
  239.7 23.1 %all-to-all-start.4 = ((bf16[2,512,128]{2,0,1:T(2,128)(2,1)}), bf16[2,512,128]{2,0,1:T(2,128)(2,1)S(1)}, u32[]{:S(2)}, u32[]{:S(2)}) async-start(bf16[2,512,128]{2,0,1:T(2,128)(2,1)} %copy.91), calls=%async_computation.4 | async-start | bytes 524288 | tf_op jit(solution)/shard_map/all_to_all | solution.py:139
  253.0 67.0 %copy-start.5 = (bf16[1,512,128]{2,1,0:T(8,128)(2,1)S(1)}, bf16[1,512,128]{2,1,0:T(8,128)(2,1)}, u32[]{:S(2)}) copy-start(bf16[1,512,128]{2,1,0:T(8,128)(2,1)} %param.5) | copy-start | bytes 393220
  262.8 19.5 %all-to-all-start.3 = ((bf16[2,512,128]{2,0,1:T(2,128)(2,1)}), bf16[2,512,128]{2,0,1:T(2,128)(2,1)S(1)}, u32[]{:S(2)}, u32[]{:S(2)}) async-start(bf16[2,512,128]{2,0,1:T(2,128)(2,1)} %copy.88), calls=%async_computation.3 | async-start | bytes 524288 | tf_op jit(solution)/shard_map/all_to_all | solution.py:136
  282.3 19.5 %all-to-all-start.11 = ((bf16[32,16,256]{2,1,0:T(8,128)(2,1)}), bf16[32,16,256]{2,1,0:T(8,128)(2,1)S(1)}, u32[]{:S(2)}, u32[]{:S(2)}) async-start(bf16[32,16,256]{2,1,0:T(8,128)(2,1)} %copy.119), calls=%async_computation.12 | async-start | bytes 524288 | tf_op jit(solution)/shard_map/all_to_all | solution.py:150
  301.8 18.2 %all-to-all-start.5 = ((bf16[32,16,128]{2,1,0:T(8,128)(2,1)}), bf16[32,16,128]{2,1,0:T(8,128)(2,1)S(1)}, u32[]{:S(2)}, u32[]{:S(2)}) async-start(bf16[32,16,128]{2,1,0:T(8,128)(2,1)} %copy.94), calls=%async_computation.5 | async-start | bytes 262144 | tf_op jit(solution)/shard_map/all_to_all | solution.py:150
  307.6 58.1 %all-reduce.2.cloned.1.call-start = ((), (), s32[]{:S(2)}) async-start(), calls=%async_computation.14 | async-start | bytes 262144 | tf_op jit(solution)/shard_map/psum | solution.py:200
  308.4 113.9 %reduce-scatter.2.cloned.1.call-start = ((), (), s32[]{:S(2)}) async-start(), calls=%async_computation.13 | async-start | bytes 5242880 | tf_op jit(solution)/shard_map/reduce_scatter | solution.py:180
  320.0 3.3 copy-start.3
Sparse Core Ops, SparseCore 0:
  10.1 59.0 all-gather.2
  311.4 54.2 all-reduce.1
  369.3 52.8 reduce-scatter.1
where the time goes:
time: 433 us; the launch traced here: 429 us
  waiting for transfers between devices  221 us (51%)
  starting transfers between devices  78.1 us (18%)
  matrix products  59 us (14%)
  blocking collectives  30.7 us (7%)
  local copies, waits for them, and re-layouts  17.2 us (4%)
  between operations  14.6 us (3%)
  other arithmetic  8.43 us (2%)
    reduce_scatter x1, waiting for transfers between devices, per_device(): lax.psum_scatter(partial_sum.astype(jnp.bfloat16), 'tensor', scatter_dime...  55 us
    dot_general x32, matrix products, apply(): return jnp.einsum(form, left, right, precision=HIGHEST)  47.5 us
    psum x1, waiting for transfers between devices, per_device(): lax.psum(result[:, width:].astype(jnp.bfloat16), 'dp').astype(jnp.float32)  41.7 us
    all_to_all x1, blocking collectives, forward_transform(): lax.all_to_all(signal.reshape(count, length // count, width).astype(jnp.b...  30.7 us
    all_to_all x2, waiting for transfers between devices, forward_transform(): lax.all_to_all(for_sending(mixed_imag), 'seq', split_axis=0, concat_axis=...  24.4 us
    all_to_all x2, waiting for transfers between devices, inverse_transform(): lax.all_to_all(for_sending(data_real), 'seq', split_axis=1, concat_axis=0...  23.5 us
    all_to_all x2, waiting for transfers between devices, inverse_transform(): lax.all_to_all(for_sending(signal), 'seq', split_axis=0, concat_axis=0, t...  23.1 us
    all_to_all x2, waiting for transfers between devices, forward_transform(): lax.all_to_all(for_sending(mixed_real), 'seq', split_axis=0, concat_axis=...  22.7 us
  transfers between devices with their start and end apart: 14, of which 13 were waited for; matrix products, arithmetic and copies ran while one was open for 12% of the time, Pallas kernels for 0%

commit v1 on v0

--- a/solution.py
+++ b/solution.py
@@ -115,8 +115,14 @@
     mixed_real = jnp.einsum("ka,arc->krc", cos_t, pieces, precision=HIGHEST)
     mixed_imag = jnp.einsum("ka,arc->krc", sin_t, pieces, precision=HIGHEST)
     mixed_real, mixed_imag = (
-        lax.all_to_all(
-            for_sending(mixed_real), "seq", split_axis=0, concat_axis=1, tiled=True
+        jnp.concatenate(
+            lax.all_to_all(
+                jnp.stack(jnp.split(for_sending(mixed_real), lax.axis_size("seq"), axis=0)),
+                "seq",
+                0,
+                0,
+            ),
+            axis=1,
         ).astype(mixed_real.dtype),
         lax.all_to_all(
             for_sending(mixed_imag), "seq", split_axis=0, concat_axis=1, tiled=True

time: 433 us -> 456 us (1.053)
  local copies, waits for them, and re-layouts: 17.2 us -> 55.2 us
  blocking collectives: 30.7 us -> 0 us
  starting transfers between devices: 78.1 us -> 105 us
  waiting for transfers between devices: 221 us -> 207 us
  other arithmetic: 8.43 us -> 15.8 us
  matrix products: 59 us -> 53.5 us
    unnamed x12 -> x92, local copies, waits for them, and re-layouts: 0.04 us -> 38.2 us
    all_to_all x1 -> x0, blocking collectives: 30.7 us -> none  [forward_transform(): lax.all_to_all(signal.reshape(count, length // count, width).astype(jnp.b...]
    all_to_all x2, waiting for transfers between devices: 24.4 us -> 0.01 us  [forward_transform(): lax.all_to_all(for_sending(mixed_imag), 'seq', split_axis=0, concat_axis=...]
    all_to_all x1 -> x2, starting transfers between devices: 9.78 us -> 26.4 us  [forward_transform(): lax.all_to_all(signal.reshape(count, length // count, width).astype(jnp.b...]
    all_to_all x2, starting transfers between devices: 10.5 us -> 25.1 us  [forward_transform(): lax.all_to_all(jnp.stack(jnp.split(for_sending(mixed_real), lax.axis_size...]
    all_to_all x1 -> x2, waiting for transfers between devices: 9.62 us -> 21.5 us  [forward_transform(): lax.all_to_all(signal.reshape(count, length // count, width).astype(jnp.b...]
    sub x0 -> x2, other arithmetic: none -> 5.45 us  [local_forward(): data_real * cos_t - data_imag * sin_t]
    dot_general x32, matrix products: 47.5 us -> 42.1 us  [apply(): return jnp.einsum(form, left, right, precision=HIGHEST)]
  transfers between devices with their start and end apart: 14 -> 15, of which waited for: 13 -> 12; matrix products, arithmetic and copies ran while one was open for 12% -> 20% of each run, Pallas kernels for 0% -> 0%
where the time goes in v1:
time: 456 us; the launch traced here: 451 us
  waiting for transfers between devices  207 us (45%)
  starting transfers between devices  105 us (23%)
  local copies, waits for them, and re-layouts  55.2 us (12%)
  matrix products  53.5 us (12%)
  other arithmetic  15.8 us (3%)
  between operations  14.7 us (3%)
    reduce_scatter x1, waiting for transfers between devices, per_device(): lax.psum_scatter(partial_sum.astype(jnp.bfloat16), 'tensor', scatter_dime...  55 us
    dot_general x32, matrix products, apply(): return jnp.einsum(form, left, right, precision=HIGHEST)  42.1 us
    psum x1, waiting for transfers between devices, per_device(): lax.psum(result[:, width:].astype(jnp.bfloat16), 'dp').astype(jnp.float32)  41.7 us
    unnamed x92, local copies, waits for them, and re-layouts  38.2 us
    all_to_all x2, starting transfers between devices, forward_transform(): lax.all_to_all(signal.reshape(count, length // count, width).astype(jnp.b...  26.4 us
    all_to_all x2, starting transfers between devices, forward_transform(): lax.all_to_all(jnp.stack(jnp.split(for_sending(mixed_real), lax.axis_size...  25.1 us
    all_to_all x2, waiting for transfers between devices, inverse_transform(): lax.all_to_all(for_sending(data_real), 'seq', split_axis=1, concat_axis=0...  23.4 us
    all_to_all x2, waiting for transfers between devices, inverse_transform(): lax.all_to_all(for_sending(signal), 'seq', split_axis=0, concat_axis=0, t...  23 us
  transfers between devices with their start and end apart: 15, of which 12 were waited for; matrix products, arithmetic and copies ran while one was open for 20% of the time, Pallas kernels for 0%

profile of v1, /device:TPU:1, one launch (start us, length us, event | category | flops | bytes accessed | tf_op | source)
XLA Modules:
  0.0 451.2 jit_solution(15415048442015804878)
XLA Ops:
  7.2 1.1 convert.16
  8.2 1.6 pad_maximum_fusion.6
  9.9 17.2 %all-to-all-start = ((bf16[32,16,256]{2,1,0:T(8,128)(2,1)}), bf16[32,16,256]{2,1,0:T(8,128)(2,1)S(1)}, u32[]{:S(2)}, u32[]{:S(2)}) async-start(bf16[32,16,256]{2,1,0:T(8,128)(2,1)} %bitcast.3), calls=%async_computation | async-start | bytes 524288 | tf_op jit(solution)/shard_map/all_to_all | solution.py:105
  27.9 12.9 %all-to-all-done = bf16[32,16,256]{2,1,0:T(8,128)(2,1)S(1)} async-done(((bf16[32,16,256]{2,1,0:T(8,128)(2,1)}), bf16[32,16,256]{2,1,0:T(8,128)(2,1)S(1)}, u32[]{:S(2)}, u32[]{:S(2)}) %all-to-all-start) | async-done | bytes 262176 | tf_op jit(solution)/shard_map/all_to_all | solution.py:105
  41.5 1.1 copy.84
  42.6 5.8 %all-to-all-start.2 = ((bf16[64,16,256]{2,1,0:T(8,128)(2,1)}), bf16[64,16,256]{2,1,0:T(8,128)(2,1)S(1)}, u32[]{:S(2)}, u32[]{:S(2)}) async-start(bf16[64,16,256]{2,1,0:T(8,128)(2,1)} %copy.84), calls=%async_computation.2 | async-start | bytes 1048576 | tf_op jit(solution)/shard_map/all_to_all | solution.py:127
  69.1 12.7 %all-to-all-start.1 = ((bf16[32,2,16,256]{3,1,2,0:T(2,128)(2,1)}), bf16[32,2,16,256]{3,1,2,0:T(2,128)(2,1)}, u32[]{:S(2)}, u32[]{:S(2)}) async-start(bf16[32,2,16,256]{3,1,2,0:T(2,128)(2,1)} %constant_dynamic-update-slice_fusion), calls=%async_computation.1 | async-start | bytes 1048576 | tf_op jit(solution)/shard_map/all_to_all | solution.py:119
  83.4 1.1 fusion.80
  84.7 12.9 %all-to-all-done.1 = bf16[32,2,16,256]{3,1,2,0:T(2,128)(2,1)} async-done(((bf16[32,2,16,256]{3,1,2,0:T(2,128)(2,1)}), bf16[32,2,16,256]{3,1,2,0:T(2,128)(2,1)}, u32[]{:S(2)}, u32[]{:S(2)}) %all-to-all-start.1) | async-done | bytes 524320 | tf_op jit(solution)/shard_map/all_to_all | solution.py:119
  97.5 3.0 fusion.22
  100.5 1.7 fusion.40
  102.3 1.7 fusion.36
  104.0 1.7 fusion.7
  105.7 2.1 multiply_subtract_fusion
  107.8 2.6 fusion.34
  110.4 4.2 fusion.70
  114.6 9.2 %all-to-all-start.6 = ((bf16[32,16,128]{2,1,0:T(8,128)(2,1)}), bf16[32,16,128]{2,1,0:T(8,128)(2,1)S(1)}, u32[]{:S(2)}, u32[]{:S(2)}) async-start(bf16[32,16,128]{2,1,0:T(8,128)(2,1)} %bitcast.533), calls=%async_computation.7 | async-start | bytes 262144 | tf_op jit(solution)/shard_map/all_to_all | solution.py:105
  123.8 3.8 fusion.5
  127.7 8.6 %all-to-all-done.6 = bf16[32,16,128]{2,1,0:T(8,128)(2,1)S(1)} async-done(((bf16[32,16,128]{2,1,0:T(8,128)(2,1)}), bf16[32,16,128]{2,1,0:T(8,128)(2,1)S(1)}, u32[]{:S(2)}, u32[]{:S(2)}) %all-to-all-start.6) | async-done | bytes 131104 | tf_op jit(solution)/shard_map/all_to_all | solution.py:105
  137.6 4.6 %all-to-all-start.8 = ((bf16[64,16,128]{2,1,0:T(8,128)(2,1)}), bf16[64,16,128]{2,1,0:T(8,128)(2,1)}, u32[]{:S(2)}, u32[]{:S(2)}) async-start(bf16[64,16,128]{2,1,0:T(8,128)(2,1)} %copy.111), calls=%async_computation.9 | async-start | bytes 524288 | tf_op jit(solution)/shard_map/all_to_all | solution.py:127
  162.1 12.3 %all-to-all-start.7 = ((bf16[32,2,16,128]{3,1,2,0:T(2,128)(2,1)}), bf16[32,2,16,128]{3,1,2,0:T(2,128)(2,1)}, u32[]{:S(2)}, u32[]{:S(2)}) async-start(bf16[32,2,16,128]{3,1,2,0:T(2,128)(2,1)} %constant_dynamic-update-slice_fusion.32), calls=%async_computation.8 | async-start | bytes 524288 | tf_op jit(solution)/shard_map/all_to_all | solution.py:119
  174.5 1.6 fusion.30
  176.1 1.6 fusion.4
  177.8 1.8 convert.20
  179.6 8.6 %all-to-all-done.7 = bf16[32,2,16,128]{3,1,2,0:T(2,128)(2,1)} async-done(((bf16[32,2,16,128]{3,1,2,0:T(2,128)(2,1)}), bf16[32,2,16,128]{3,1,2,0:T(2,128)(2,1)}, u32[]{:S(2)}, u32[]{:S(2)}) %all-to-all-start.7) | async-done | bytes 262176 | tf_op jit(solution)/shard_map/all_to_all | solution.py:119
  188.2 2.5 fusion.44
  190.7 0.9 fusion.60
  191.6 0.9 fusion.56
  192.6 1.0 fusion.12
  193.5 1.1 multiply_subtract_fusion.3
  194.6 0.9 fusion.54
  195.5 0.9 fusion.50
  196.4 0.9 fusion.9
  197.4 1.2 multiply_subtract_fusion.2
  199.3 1.1 fusion.42
  200.3 1.1 fusion.43
  201.4 1.1 convolution_add_fusion.1
  202.5 1.7 add_bitcast_fusion
  204.1 1.7 fusion.28
  205.9 1.7 fusion.24
  207.6 1.7 fusion.3
  209.3 1.7 fusion.2
  212.3 1.1 fusion.21
  213.5 1.3 copy.132
  214.8 6.3 %all-to-all-start.10 = ((bf16[2,512,256]{2,0,1:T(2,128)(2,1)}), bf16[2,512,256]{2,0,1:T(2,128)(2,1)S(1)}, u32[]{:S(2)}, u32[]{:S(2)}) async-start(bf16[2,512,256]{2,0,1:T(2,128)(2,1)} %copy.132), calls=%async_computation.11 | async-start | bytes 1048576 | tf_op jit(solution)/shard_map/all_to_all | solution.py:145
  221.1 2.4 copy.129
  226.3 10.5 %all-to-all-done.10 = bf16[2,512,256]{2,0,1:T(2,128)(2,1)S(1)} async-done(((bf16[2,512,256]{2,0,1:T(2,128)(2,1)}), bf16[2,512,256]{2,0,1:T(2,128)(2,1)S(1)}, u32[]{:S(2)}, u32[]{:S(2)}) %all-to-all-start.10) | async-done | bytes 524320 | tf_op jit(solution)/shard_map/all_to_all | solution.py:145
  236.8 9.3 %all-to-all-start.9 = ((bf16[2,512,256]{2,0,1:T(2,128)(2,1)}), bf16[2,512,256]{2,0,1:T(2,128)(2,1)}, u32[]{:S(2)}, u32[]{:S(2)}) async-start(bf16[2,512,256]{2,0,1:T(2,128)(2,1)} %copy.129), calls=%async_computation.10 | async-start | bytes 1048576 | tf_op jit(solution)/shard_map/all_to_all | solution.py:142
  249.5 1.0 copy.105
  250.5 11.6 %all-to-all-done.9 = bf16[2,512,256]{2,0,1:T(2,128)(2,1)} async-done(((bf16[2,512,256]{2,0,1:T(2,128)(2,1)}), bf16[2,512,256]{2,0,1:T(2,128)(2,1)}, u32[]{:S(2)}, u32[]{:S(2)}) %all-to-all-start.9) | async-done | bytes 524320 | tf_op jit(solution)/shard_map/all_to_all | solution.py:142
  262.0 9.3 %all-to-all-start.4 = ((bf16[2,512,128]{2,0,1:T(2,128)(2,1)}), bf16[2,512,128]{2,0,1:T(2,128)(2,1)S(1)}, u32[]{:S(2)}, u32[]{:S(2)}) async-start(bf16[2,512,128]{2,0,1:T(2,128)(2,1)} %copy.105), calls=%async_computation.4 | async-start | bytes 524288 | tf_op jit(solution)/shard_map/all_to_all | solution.py:145
  271.3 1.0 copy.102
  273.1 1.1 copy.130
  275.0 9.9 %all-to-all-done.4 = bf16[2,512,128]{2,0,1:T(2,128)(2,1)S(1)} async-done(((bf16[2,512,128]{2,0,1:T(2,128)(2,1)}), bf16[2,512,128]{2,0,1:T(2,128)(2,1)S(1)}, u32[]{:S(2)}, u32[]{:S(2)}) %all-to-all-start.4) | async-done | bytes 262176 | tf_op jit(solution)/shard_map/all_to_all | solution.py:145
  284.9 5.8 %all-to-all-start.3 = ((bf16[2,512,128]{2,0,1:T(2,128)(2,1)}), bf16[2,512,128]{2,0,1:T(2,128)(2,1)S(1)}, u32[]{:S(2)}, u32[]{:S(2)}) async-start(bf16[2,512,128]{2,0,1:T(2,128)(2,1)} %copy.102), calls=%async_computation.3 | async-start | bytes 524288 | tf_op jit(solution)/shard_map/all_to_all | solution.py:142
  292.5 11.9 %all-to-all-done.3 = bf16[2,512,128]{2,0,1:T(2,128)(2,1)S(1)} async-done(((bf16[2,512,128]{2,0,1:T(2,128)(2,1)}), bf16[2,512,128]{2,0,1:T(2,128)(2,1)S(1)}, u32[]{:S(2)}, u32[]{:S(2)}) %all-to-all-start.3) | async-done | bytes 262176 | tf_op jit(solution)/shard_map/all_to_all | solution.py:142
  304.4 6.1 %all-to-all-start.11 = ((bf16[32,16,256]{2,1,0:T(8,128)(2,1)}), bf16[32,16,256]{2,1,0:T(8,128)(2,1)S(1)}, u32[]{:S(2)}, u32[]{:S(2)}) async-start(bf16[32,16,256]{2,1,0:T(8,128)(2,1)} %copy.135), calls=%async_computation.12 | async-start | bytes 524288 | tf_op jit(solution)/shard_map/all_to_all | solution.py:156
  312.6 11.5 %all-to-all-done.11 = bf16[32,16,256]{2,1,0:T(8,128)(2,1)S(1)} async-done(((bf16[32,16,256]{2,1,0:T(8,128)(2,1)}), bf16[32,16,256]{2,1,0:T(8,128)(2,1)S(1)}, u32[]{:S(2)}, u32[]{:S(2)}) %all-to-all-start.11) | async-done | bytes 262176 | tf_op jit(solution)/shard_map/all_to_all | solution.py:156
  324.0 5.8 %all-to-all-start.5 = ((bf16[32,16,128]{2,1,0:T(8,128)(2,1)}), bf16[32,16,128]{2,1,0:T(8,128)(2,1)S(1)}, u32[]{:S(2)}, u32[]{:S(2)}) async-start(bf16[32,16,128]{2,1,0:T(8,128)(2,1)} %copy.108), calls=%async_computation.5 | async-start | bytes 262144 | tf_op jit(solution)/shard_map/all_to_all | solution.py:156
  330.7 11.5 %all-to-all-done.5 = bf16[32,16,128]{2,1,0:T(8,128)(2,1)S(1)} async-done(((bf16[32,16,128]{2,1,0:T(8,128)(2,1)}), bf16[32,16,128]{2,1,0:T(8,128)(2,1)S(1)}, u32[]{:S(2)}, u32[]{:S(2)}) %all-to-all-start.5) | async-done | bytes 131104 | tf_op jit(solution)/shard_map/all_to_all | solution.py:156
  342.2 3.2 convolution_convert_fusion
  346.2 41.7 %all-reduce.2.cloned.1.call-done = bf16[512,128]{1,0:T(8,128)(2,1)} async-done(((bf16[512,128]{1,0:T(8,128)(2,1)}), bf16[512,128]{1,0:T(8,128)(2,1)}) %all-reduce.2.cloned.1.call-update) | async-done | bytes 131088 | tf_op jit(solution)/shard_map/psum | solution.py:206
  387.9 1.6 convert_element_type.297
  389.5 55.0 %reduce-scatter.2.cloned.1.call-done = bf16[512,1024]{1,0:T(8,128)(2,1)} async-done(((bf16[512,4096]{1,0:T(8,128)(2,1)}), bf16[512,1024]{1,0:T(8,128)(2,1)}) %reduce-scatter.2.cloned.1.call-update) | async-done | bytes 1048592 | tf_op jit(solution)/shard_map/reduce_scatter | solution.py:186
  (145 shorter events, 59.8 us)
Async XLA Ops:
  7.2 103.3 %copy-start = (bf16[128,4096]{1,0:T(8,128)(2,1)S(1)}, bf16[128,4096]{1,0:T(8,128)(2,1)}, u32[]{:S(2)}) copy-start(bf16[128,4096]{1,0:T(8,128)(2,1)} %param.8) | copy-start | bytes 3145732
  9.9 30.9 %all-to-all-start = ((bf16[32,16,256]{2,1,0:T(8,128)(2,1)}), bf16[32,16,256]{2,1,0:T(8,128)(2,1)S(1)}, u32[]{:S(2)}, u32[]{:S(2)}) async-start(bf16[32,16,256]{2,1,0:T(8,128)(2,1)} %bitcast.3), calls=%async_computation | async-start | bytes 524288 | tf_op jit(solution)/shard_map/all_to_all | solution.py:105
  27.1 83.3 %all-gather.3.cloned.1.call-start = ((), (), s32[]{:S(2)}) async-start(), calls=%async_computation.15 | async-start | bytes 5242880 | tf_op jit(solution)/shard_map/all_gather | solution.py:190
  42.6 26.5 %all-to-all-start.2 = ((bf16[64,16,256]{2,1,0:T(8,128)(2,1)}), bf16[64,16,256]{2,1,0:T(8,128)(2,1)S(1)}, u32[]{:S(2)}, u32[]{:S(2)}) async-start(bf16[64,16,256]{2,1,0:T(8,128)(2,1)} %copy.84), calls=%async_computation.2 | async-start | bytes 1048576 | tf_op jit(solution)/shard_map/all_to_all | solution.py:127
  69.1 28.5 %all-to-all-start.1 = ((bf16[32,2,16,256]{3,1,2,0:T(2,128)(2,1)}), bf16[32,2,16,256]{3,1,2,0:T(2,128)(2,1)}, u32[]{:S(2)}, u32[]{:S(2)}) async-start(bf16[32,2,16,256]{3,1,2,0:T(2,128)(2,1)} %constant_dynamic-update-slice_fusion), calls=%async_computation.1 | async-start | bytes 1048576 | tf_op jit(solution)/shard_map/all_to_all | solution.py:119
  81.9 0.8 copy-start.7
  81.9 0.8 copy-start.10
  84.5 19.5 %copy-start.1 = (f32[2,32,16]{0,2,1:T(8,128)}, f32[2,32,16]{0,2,1:T(8,128)S(1)}, u32[]{:S(2)}) copy-start(f32[2,32,16]{0,2,1:T(8,128)S(1)} %get-tuple-element.29) | copy-start | bytes 12292
  100.5 5.2 %copy-start.8 = (f32[32,16]{0,1:T(8,128)S(1)}, f32[32,16]{0,1:T(8,128)}, u32[]{:S(2)}) copy-start(f32[32,16]{0,1:T(8,128)} %copy-done.7) | copy-start | bytes 6148
  100.5 5.2 %copy-start.11 = (f32[32,16]{0,1:T(8,128)S(1)}, f32[32,16]{0,1:T(8,128)}, u32[]{:S(2)}) copy-start(f32[32,16]{0,1:T(8,128)} %copy-done.10) | copy-start | bytes 6148
  105.7 4.7 %copy-start.4 = (bf16[1,512,128]{2,1,0:T(8,128)(2,1)S(1)}, bf16[1,512,128]{2,1,0:T(8,128)(2,1)}, u32[]{:S(2)}) copy-start(bf16[1,512,128]{2,1,0:T(8,128)(2,1)} %param.5) | copy-start | bytes 393220
  114.6 21.6 %all-to-all-start.6 = ((bf16[32,16,128]{2,1,0:T(8,128)(2,1)}), bf16[32,16,128]{2,1,0:T(8,128)(2,1)S(1)}, u32[]{:S(2)}, u32[]{:S(2)}) async-start(bf16[32,16,128]{2,1,0:T(8,128)(2,1)} %bitcast.533), calls=%async_computation.7 | async-start | bytes 262144 | tf_op jit(solution)/shard_map/all_to_all | solution.py:105
  137.6 24.5 %all-to-all-start.8 = ((bf16[64,16,128]{2,1,0:T(8,128)(2,1)}), bf16[64,16,128]{2,1,0:T(8,128)(2,1)}, u32[]{:S(2)}, u32[]{:S(2)}) async-start(bf16[64,16,128]{2,1,0:T(8,128)(2,1)} %copy.111), calls=%async_computation.9 | async-start | bytes 524288 | tf_op jit(solution)/shard_map/all_to_all | solution.py:127
  162.1 26.0 %all-to-all-start.7 = ((bf16[32,2,16,128]{3,1,2,0:T(2,128)(2,1)}), bf16[32,2,16,128]{3,1,2,0:T(2,128)(2,1)}, u32[]{:S(2)}, u32[]{:S(2)}) async-start(bf16[32,2,16,128]{3,1,2,0:T(2,128)(2,1)} %constant_dynamic-update-slice_fusion.32), calls=%async_computation.8 | async-start | bytes 524288 | tf_op jit(solution)/shard_map/all_to_all | solution.py:119
  177.7 15.8 %copy-start.9 = (f32[32,16]{0,1:T(8,128)S(1)}, f32[32,16]{0,1:T(8,128)}, u32[]{:S(2)}) copy-start(f32[32,16]{0,1:T(8,128)} %copy-done.7) | copy-start | bytes 6148
  177.8 15.8 %copy-start.12 = (f32[32,16]{0,1:T(8,128)S(1)}, f32[32,16]{0,1:T(8,128)}, u32[]{:S(2)}) copy-start(f32[32,16]{0,1:T(8,128)} %copy-done.10) | copy-start | bytes 6148
  192.5 4.8 %copy-start.2 = (f32[2,32,16,256]{3,2,1,0:T(8,128)S(1)}, f32[2,32,16,256]{3,2,1,0:T(8,128)}, u32[]{:S(2)}) copy-start(f32[2,32,16,256]{3,2,1,0:T(8,128)} %fusion.5) | copy-start | bytes 3145732
  198.6 3.8 copy-start.6
  209.3 3.0 copy-start.13
  209.3 3.0 copy-start.14
  214.8 22.0 %all-to-all-start.10 = ((bf16[2,512,256]{2,0,1:T(2,128)(2,1)}), bf16[2,512,256]{2,0,1:T(2,128)(2,1)S(1)}, u32[]{:S(2)}, u32[]{:S(2)}) async-start(bf16[2,512,256]{2,0,1:T(2,128)(2,1)} %copy.132), calls=%async_computation.11 | async-start | bytes 1048576 | tf_op jit(solution)/shard_map/all_to_all | solution.py:145
  236.8 25.2 %all-to-all-start.9 = ((bf16[2,512,256]{2,0,1:T(2,128)(2,1)}), bf16[2,512,256]{2,0,1:T(2,128)(2,1)}, u32[]{:S(2)}, u32[]{:S(2)}) async-start(bf16[2,512,256]{2,0,1:T(2,128)(2,1)} %copy.129), calls=%async_computation.10 | async-start | bytes 1048576 | tf_op jit(solution)/shard_map/all_to_all | solution.py:142
  262.0 22.9 %all-to-all-start.4 = ((bf16[2,512,128]{2,0,1:T(2,128)(2,1)}), bf16[2,512,128]{2,0,1:T(2,128)(2,1)S(1)}, u32[]{:S(2)}, u32[]{:S(2)}) async-start(bf16[2,512,128]{2,0,1:T(2,128)(2,1)} %copy.105), calls=%async_computation.4 | async-start | bytes 524288 | tf_op jit(solution)/shard_map/all_to_all | solution.py:145
  275.0 67.3 %copy-start.5 = (bf16[1,512,128]{2,1,0:T(8,128)(2,1)S(1)}, bf16[1,512,128]{2,1,0:T(8,128)(2,1)}, u32[]{:S(2)}) copy-start(bf16[1,512,128]{2,1,0:T(8,128)(2,1)} %param.5) | copy-start | bytes 393220
  284.9 19.5 %all-to-all-start.3 = ((bf16[2,512,128]{2,0,1:T(2,128)(2,1)}), bf16[2,512,128]{2,0,1:T(2,128)(2,1)S(1)}, u32[]{:S(2)}, u32[]{:S(2)}) async-start(bf16[2,512,128]{2,0,1:T(2,128)(2,1)} %copy.102), calls=%async_computation.3 | async-start | bytes 524288 | tf_op jit(solution)/shard_map/all_to_all | solution.py:142
  304.4 19.6 %all-to-all-start.11 = ((bf16[32,16,256]{2,1,0:T(8,128)(2,1)}), bf16[32,16,256]{2,1,0:T(8,128)(2,1)S(1)}, u32[]{:S(2)}, u32[]{:S(2)}) async-start(bf16[32,16,256]{2,1,0:T(8,128)(2,1)} %copy.135), calls=%async_computation.12 | async-start | bytes 524288 | tf_op jit(solution)/shard_map/all_to_all | solution.py:156
  324.0 18.2 %all-to-all-start.5 = ((bf16[32,16,128]{2,1,0:T(8,128)(2,1)}), bf16[32,16,128]{2,1,0:T(8,128)(2,1)S(1)}, u32[]{:S(2)}, u32[]{:S(2)}) async-start(bf16[32,16,128]{2,1,0:T(8,128)(2,1)} %copy.108), calls=%async_computation.5 | async-start | bytes 262144 | tf_op jit(solution)/shard_map/all_to_all | solution.py:156
  329.9 58.0 %all-reduce.2.cloned.1.call-start = ((), (), s32[]{:S(2)}) async-start(), calls=%async_computation.14 | async-start | bytes 262144 | tf_op jit(solution)/shard_map/psum | solution.py:206
  330.7 113.8 %reduce-scatter.2.cloned.1.call-start = ((), (), s32[]{:S(2)}) async-start(), calls=%async_computation.13 | async-start | bytes 5242880 | tf_op jit(solution)/shard_map/reduce_scatter | solution.py:186
  342.2 3.3 copy-start.3
Sparse Core Ops, SparseCore 0:
  30.1 53.9 all-gather.2
  333.6 54.1 all-reduce.1
  391.5 52.8 reduce-scatter.1
